TPU v7x, 256 devices: a whole 4x4x8 slice. The times are simulated.
256 devices in a mesh: row: 8 (over z), col: 32 (over y, x, core).
Axes of the slice: x: 4, y: 4, z: 8, core: 2. Of those that a mesh axis runs over, the one named last changes fastest.
Arguments:
- factor_tiles: bfloat16 [3, 96, 64, 2048], P(None, 'row', None, 'col'), may hold values from -0.3125 to 0.3125
- tile_row: int32 [3, 96, 32], P(None, 'row', 'col'), may hold values from 0 to 63
- tile_col: int32 [3, 96, 32], P(None, 'row', 'col'), may hold values from 0 to 15
- right_sides: float32 [4, 512, 64, 128], P(None, ('col', 'row')), may hold values from -6 to 6
- diag_inverse: float32 [4, 64, 32768], P(None, None, ('col', 'row')), as said below
Outputs:
- preconditioned: float32 [4, 512, 64, 128], P(None, ('col', 'row'))
Inputs may be any that keep to these rules, and one draw needn't show every extreme that they name: `tile_row`: a block row within its row group. `tile_col`: a block column within its column group. `diag_inverse`: diagonal entries of every block between 0.5 and 2.
All inputs are finite; a program needn't handle non-finite values.
Results may differ from a plain program's by a relative error of at most 0.025.
Values may be sent and summed in bfloat16 or wider, within the bound.
A program may use at most 64 MiB of HBM per device.

v0:
```python
import jax
import jax.numpy as jnp
from jax import lax
from jax.sharding import PartitionSpec as P


def apply_inverse(inverse, vector, transposed):
    matrix = inverse.reshape(inverse.shape[0], -1, inverse.shape[0])
    if transposed:
        return jnp.einsum("cir,irn->icn", matrix, vector, precision=lax.Precision.HIGHEST)
    return jnp.einsum("cir,icn->irn", matrix, vector, precision=lax.Precision.HIGHEST)


def solve_all(factor_tiles, tile_row, tile_col, right_sides, diag_inverse):
    levels = factor_tiles.shape[0]
    rows_dev = right_sides.shape[1]
    group_rows = rows_dev * lax.axis_size("row")
    row_ids = tile_row[:, :, 0]
    col_ids = tile_col[:, :, 0]
    current = apply_inverse(diag_inverse[0], right_sides[0], False)
    solved = [current]
    for section_no in range(1, levels + 1):
        gathered = lax.all_gather(current.astype(jnp.bfloat16), "row", axis=0, tiled=True)
        picked = gathered[col_ids[section_no - 1]]
        products = jnp.einsum(
            "tab,tbn->tan", factor_tiles[section_no - 1], picked, preferred_element_type=jnp.float32
        )
        targets = row_ids[section_no - 1]

        def term(offset, length, products=products, targets=targets):
            places = jnp.arange(length, dtype=jnp.int32)
            select = (targets[:, None] == places[None, :]).astype(jnp.float32)
            return jnp.einsum("tq,tan->qan", select, products, precision=lax.Precision.HIGHEST)

        row_sums = lax.psum_scatter(
            term(jnp.int32(0), lax.axis_size("col") * rows_dev).astype(jnp.bfloat16),
            "col",
            scatter_dimension=0,
            tiled=True,
        ).astype(jnp.float32)
        current = apply_inverse(diag_inverse[section_no], right_sides[section_no] - row_sums, False)
        solved.append(current)
    current = apply_inverse(diag_inverse[levels], solved[levels], True)
    result = [current]
    columns_here = jnp.arange(group_rows, dtype=jnp.int32)
    for section_no in range(levels - 1, -1, -1):
        everyone = lax.all_gather(current.astype(jnp.bfloat16), "col", axis=0, tiled=True)
        picked = everyone[row_ids[section_no]]
        spread = jnp.einsum(
            "tab,tan->tbn", factor_tiles[section_no], picked, preferred_element_type=jnp.float32
        )
        select = (col_ids[section_no][:, None] == columns_here[None, :]).astype(jnp.float32)
        column_sums = jnp.einsum("tj,tbn->jbn", select, spread, precision=lax.Precision.HIGHEST)
        received = lax.psum_scatter(
            column_sums.astype(jnp.bfloat16), "row", scatter_dimension=0, tiled=True
        ).astype(jnp.float32)
        current = apply_inverse(diag_inverse[section_no], solved[section_no] - received, True)
        result.insert(0, current)
    return jnp.stack(result)


def on_device(factor_tiles, tile_row, tile_col, right_sides, diag_inverse):
    return solve_all(factor_tiles, tile_row, tile_col, right_sides, diag_inverse)


def solution(mesh):
    return jax.shard_map(
        on_device,
        mesh=mesh,
        in_specs=(
            P(None, "row", None, "col"),
            P(None, "row", "col"),
            P(None, "row", "col"),
            P(None, ("col", "row"), None, None),
            P(None, None, ("col", "row")),
        ),
        out_specs=P(None, ("col", "row"), None, None),
        check_vma=False,
    )
```

profile of v0, /device:TPU:2, one launch (start us, length us, event | category | flops | bytes accessed | tf_op | source)
XLA Modules:
  0.0 630.8 jit_solution(13500943562827002383)
XLA Ops:
  6.5 0.9 fusion.66
  7.5 1.0 fusion.67
  8.6 28.6 %all_gather.18 = bf16[16,64,128]{2,1,0:T(8,128)(2,1)S(1)} all-gather(bf16[2,64,128]{2,1,0:T(8,128)(2,1)S(1)} %get-tuple-element.21), channel_id=1, replica_groups=mesh['row'=8,'col'=32] {'row'}, dimensions={0}, use_global_device_ids=true | all-gather | bytes 294912 | tf_op jit(solution)/shard_map/all_gather | solution.py:23
  37.1 0.7 fusion.62
  37.8 0.7 slice_bitcast_fusion
  38.5 0.6 gather_fusion
  39.1 0.2 convolution_bitcast_fusion.2
  39.3 1.1 convolution_convert_fusion.2
  40.4 1.7 copy.47
  42.3 84.0 %reduce-scatter.7.cloned.1.call-done = bf16[2,64,128]{2,1,0:T(8,128)(2,1)} async-done(((bf16[64,64,128]{2,1,0:T(8,128)(2,1)}), bf16[2,64,128]{2,1,0:T(8,128)(2,1)}) %reduce-scatter.7.cloned.1.call-update) | async-done | bytes 32784 | tf_op jit(solution)/shard_map/reduce_scatter | solution.py:35
  126.3 1.0 fusion.68
  127.3 26.2 %all_gather.19 = bf16[16,64,128]{2,1,0:T(8,128)(2,1)S(1)} all-gather(bf16[2,64,128]{2,1,0:T(8,128)(2,1)S(1)} %get-tuple-element.23), channel_id=1, replica_groups=mesh['row'=8,'col'=32] {'row'}, dimensions={0}, use_global_device_ids=true | all-gather | bytes 294912 | tf_op jit(solution)/shard_map/all_gather | solution.py:23
  153.5 0.6 gather_fusion.1
  154.1 0.2 convolution_bitcast_fusion.1
  154.3 1.1 convolution_convert_fusion.1
  155.4 1.7 copy.50
  157.3 83.2 %reduce-scatter.9.cloned.1.call-done = bf16[2,64,128]{2,1,0:T(8,128)(2,1)} async-done(((bf16[64,64,128]{2,1,0:T(8,128)(2,1)}), bf16[2,64,128]{2,1,0:T(8,128)(2,1)}) %reduce-scatter.9.cloned.1.call-update) | async-done | bytes 32784 | tf_op jit(solution)/shard_map/reduce_scatter | solution.py:35
  240.5 1.0 fusion.69
  241.5 26.3 %all_gather.20 = bf16[16,64,128]{2,1,0:T(8,128)(2,1)S(1)} all-gather(bf16[2,64,128]{2,1,0:T(8,128)(2,1)S(1)} %get-tuple-element.25), channel_id=1, replica_groups=mesh['row'=8,'col'=32] {'row'}, dimensions={0}, use_global_device_ids=true | all-gather | bytes 294912 | tf_op jit(solution)/shard_map/all_gather | solution.py:23
  267.8 0.6 gather_fusion.2
  268.4 0.2 convolution_bitcast_fusion
  268.6 1.1 convolution_convert_fusion
  269.7 1.7 copy.53
  271.5 83.2 %reduce-scatter.11.cloned.1.call-done = bf16[2,64,128]{2,1,0:T(8,128)(2,1)} async-done(((bf16[64,64,128]{2,1,0:T(8,128)(2,1)}), bf16[2,64,128]{2,1,0:T(8,128)(2,1)}) %reduce-scatter.11.cloned.1.call-update) | async-done | bytes 32784 | tf_op jit(solution)/shard_map/reduce_scatter | solution.py:35
  354.7 1.0 fusion.21
  355.7 0.8 bitcast_convert_fusion.2
  356.7 48.0 %all-gather.4.cloned.1.call-done = bf16[64,64,128]{2,1,0:T(8,128)(2,1)} async-done(((bf16[2,64,128]{2,1,0:T(8,128)(2,1)}), bf16[64,64,128]{2,1,0:T(8,128)(2,1)}) %all-gather.4.cloned.1.call-update) | async-done | bytes 1048592 | tf_op jit(solution)/shard_map/all_gather | solution.py:47
  404.7 1.8 gather_fusion.3
  406.5 0.3 convolution_bitcast_fusion.5
  406.7 0.6 fusion.4
  407.3 0.8 copy.95
  408.2 36.5 %reduce-scatter.13.cloned.1.call-done = bf16[2,64,128]{2,1,0:T(8,128)(2,1)} async-done(((bf16[16,64,128]{2,1,0:T(8,128)(2,1)}), bf16[2,64,128]{2,1,0:T(8,128)(2,1)}) %reduce-scatter.13.cloned.1.call-update) | async-done | bytes 32784 | tf_op jit(solution)/shard_map/reduce_scatter | solution.py:54
  444.7 1.7 bitcast_convert_fusion.1
  446.4 46.9 %all-gather.6.cloned.1.call-done = bf16[64,64,128]{2,1,0:T(8,128)(2,1)} async-done(((bf16[2,64,128]{2,1,0:T(8,128)(2,1)}), bf16[64,64,128]{2,1,0:T(8,128)(2,1)}) %all-gather.6.cloned.1.call-update) | async-done | bytes 1048592 | tf_op jit(solution)/shard_map/all_gather | solution.py:47
  493.3 1.8 gather_fusion.4
  495.1 0.3 convolution_bitcast_fusion.4
  495.4 0.6 fusion.2
  496.0 0.8 copy.94
  496.8 36.5 %reduce-scatter.15.cloned.1.call-done = bf16[2,64,128]{2,1,0:T(8,128)(2,1)} async-done(((bf16[16,64,128]{2,1,0:T(8,128)(2,1)}), bf16[2,64,128]{2,1,0:T(8,128)(2,1)}) %reduce-scatter.15.cloned.1.call-update) | async-done | bytes 32784 | tf_op jit(solution)/shard_map/reduce_scatter | solution.py:54
  533.4 1.7 bitcast_convert_fusion
  535.1 47.3 %all-gather.8.cloned.1.call-done = bf16[64,64,128]{2,1,0:T(8,128)(2,1)} async-done(((bf16[2,64,128]{2,1,0:T(8,128)(2,1)}), bf16[64,64,128]{2,1,0:T(8,128)(2,1)}) %all-gather.8.cloned.1.call-update) | async-done | bytes 1048592 | tf_op jit(solution)/shard_map/all_gather | solution.py:47
  582.4 1.8 gather_fusion.5
  584.2 0.3 convolution_bitcast_fusion.3
  584.5 0.6 fusion
  585.1 0.8 copy.93
  585.9 36.6 %reduce-scatter.17.cloned.1.call-done = bf16[2,64,128]{2,1,0:T(8,128)(2,1)} async-done(((bf16[16,64,128]{2,1,0:T(8,128)(2,1)}), bf16[2,64,128]{2,1,0:T(8,128)(2,1)}) %reduce-scatter.17.cloned.1.call-update) | async-done | bytes 32784 | tf_op jit(solution)/shard_map/reduce_scatter | solution.py:54
  622.5 1.0 convolution_bitcast_fusion.6
  623.5 0.7 pad_maximum_fusion
  (38 shorter events, 0.9 us)
Async XLA Ops:
  6.5 32.6 %copy-start = (bf16[3,12,64,64]{3,2,1,0:T(8,128)(2,1)S(1)}, bf16[3,12,64,64]{3,2,1,0:T(8,128)(2,1)}, u32[]{:S(2)}) copy-start(bf16[3,12,64,64]{3,2,1,0:T(8,128)(2,1)} %param.5) | copy-start | bytes 884740
  6.5 119.8 %reduce-scatter.7.cloned.1.call-start = ((), (), s32[]{:S(2)}) async-start(), calls=%async_computation.6 | async-start | bytes 1081344 | tf_op jit(solution)/shard_map/reduce_scatter | solution.py:35
  42.1 84.2 %copy-start.1 = (f32[4,2,64,128]{3,2,1,0:T(8,128)S(1)}, f32[4,2,64,128]{3,2,1,0:T(8,128)}, u32[]{:S(2)}) copy-start(f32[4,2,64,128]{3,2,1,0:T(8,128)} %param.8) | copy-start | bytes 786436
  42.1 198.4 %reduce-scatter.9.cloned.1.call-start = ((), (), s32[]{:S(2)}) async-start(), calls=%async_computation.7 | async-start | bytes 1081344 | tf_op jit(solution)/shard_map/reduce_scatter | solution.py:35
  157.1 197.6 %reduce-scatter.11.cloned.1.call-start = ((), (), s32[]{:S(2)}) async-start(), calls=%async_computation.8 | async-start | bytes 1081344 | tf_op jit(solution)/shard_map/reduce_scatter | solution.py:35
  271.4 85.3 %copy-start.2 = (s32[3,12,1]{1,2,0:T(1,128)S(1)}, s32[3,12,1]{1,2,0:T(1,128)}, u32[]{:S(2)}) copy-start(s32[3,12,1]{1,2,0:T(1,128)} %param.6) | copy-start | bytes 436
  271.4 85.3 %copy-start.3 = (s32[3,12,1]{1,2,0:T(1,128)S(1)}, s32[3,12,1]{1,2,0:T(1,128)}, u32[]{:S(2)}) copy-start(s32[3,12,1]{1,2,0:T(1,128)} %param.7) | copy-start | bytes 436
  271.4 133.3 %all-gather.4.cloned.1.call-start = ((), (), s32[]{:S(2)}) async-start(), calls=%async_computation.9 | async-start | bytes 1081344 | tf_op jit(solution)/shard_map/all_gather | solution.py:47
  356.6 88.1 %reduce-scatter.13.cloned.1.call-start = ((), (), s32[]{:S(2)}) async-start(), calls=%async_computation.10 | async-start | bytes 294912 | tf_op jit(solution)/shard_map/reduce_scatter | solution.py:54
  408.1 85.2 %all-gather.6.cloned.1.call-start = ((), (), s32[]{:S(2)}) async-start(), calls=%async_computation.11 | async-start | bytes 1081344 | tf_op jit(solution)/shard_map/all_gather | solution.py:47
  446.4 87.0 %reduce-scatter.15.cloned.1.call-start = ((), (), s32[]{:S(2)}) async-start(), calls=%async_computation.12 | async-start | bytes 294912 | tf_op jit(solution)/shard_map/reduce_scatter | solution.py:54
  496.8 85.7 %all-gather.8.cloned.1.call-start = ((), (), s32[]{:S(2)}) async-start(), calls=%async_computation.13 | async-start | bytes 1081344 | tf_op jit(solution)/shard_map/all_gather | solution.py:47
  535.0 87.4 %reduce-scatter.17.cloned.1.call-start = ((), (), s32[]{:S(2)}) async-start(), calls=%async_computation.14 | async-start | bytes 294912 | tf_op jit(solution)/shard_map/reduce_scatter | solution.py:54
Sparse Core Ops, SparseCore 0:
  42.2 84.0 reduce-scatter.6
  157.2 83.2 reduce-scatter.8
  271.5 83.1 reduce-scatter.10
  357.4 47.1 all-gather.3
  408.2 36.3 reduce-scatter.12
  447.1 46.1 all-gather.5
  496.9 36.4 reduce-scatter.14
  536.2 46.1 all-gather.7
  586.0 36.3 reduce-scatter.16
where the time goes:
time: 631 us
  waiting for transfers between devices  502 us (80%)
  blocking collectives  81.1 us (13%)
  local copies, waits for them, and re-layouts  16.5 us (3%)
  matrix products  15.6 us (2%)
  between operations  13.5 us (2%)
    reduce_scatter x3, waiting for transfers between devices, solve_all(): lax.psum_scatter(term(jnp.int32(0), lax.axis_size('col') * rows_dev).asty...  250 us
    all_gather x3, waiting for transfers between devices, solve_all(): lax.all_gather(current.astype(jnp.bfloat16), 'col', axis=0, tiled=True)  142 us
    reduce_scatter x3, waiting for transfers between devices, solve_all(): lax.psum_scatter(column_sums.astype(jnp.bfloat16), 'row', scatter_dimensi...  110 us
    all_gather x3, blocking collectives, solve_all(): lax.all_gather(current.astype(jnp.bfloat16), 'row', axis=0, tiled=True)  81.1 us
  transfers between devices with their start and end apart: 9, of which 9 were waited for; matrix products, arithmetic and copies ran while one was open for 0% of the time, Pallas kernels for 0%

commit v1 on v0

--- a/solution.py
+++ b/solution.py
@@ -1,7 +1,20 @@
+import functools
 import jax
 import jax.numpy as jnp
 from jax import lax
 from jax.sharding import PartitionSpec as P
+from jax.lax import all_to_all, axis_size
+
+
+def enter_wires(tile_in, ax_name):
+    right_arr = axis_size(ax_name)
+    y2 = jnp.stack([tile_in] * right_arr)
+    arr_next = all_to_all(y2, ax_name, split_axis=0, concat_axis=0)
+    placed = jnp.concatenate(arr_next, axis=0)
+    return placed
+
+
+scan_members_all_for = functools.partial(enter_wires, ax_name="col")
 
 
 def apply_inverse(inverse, vector, transposed):
@@ -44,7 +57,7 @@
     result = [current]
     columns_here = jnp.arange(group_rows, dtype=jnp.int32)
     for section_no in range(levels - 1, -1, -1):
-        everyone = lax.all_gather(current.astype(jnp.bfloat16), "col", axis=0, tiled=True)
+        everyone = scan_members_all_for(current.astype(jnp.bfloat16))
         picked = everyone[row_ids[section_no]]
         spread = jnp.einsum(
             "tab,tan->tbn", factor_tiles[section_no], picked, preferred_element_type=jnp.float32

time: 631 us -> 549 us (0.87)
  waiting for transfers between devices: 502 us -> 400 us
  starting transfers between devices: 0.34 us -> 21.1 us
    all_gather x3 -> x0, waiting for transfers between devices: 142 us -> none  [solve_all(): lax.all_gather(current.astype(jnp.bfloat16), 'col', axis=0, tiled=True)]
    all_to_all x0 -> x3, waiting for transfers between devices: none -> 48.1 us  [enter_wires(): arr_next = all_to_all(y2, ax_name, split_axis=0, concat_axis=0)]
    all_to_all x0 -> x3, starting transfers between devices: none -> 20.9 us  [enter_wires(): arr_next = all_to_all(y2, ax_name, split_axis=0, concat_axis=0)]
    reduce_scatter x3, waiting for transfers between devices: 110 us -> 101 us  [solve_all(): lax.psum_scatter(column_sums.astype(jnp.bfloat16), 'row', scatter_dimensi...]
where the time goes in v1:
time: 549 us; the launch traced here: 548 us
  waiting for transfers between devices  400 us (73%)
  blocking collectives  81.1 us (15%)
  starting transfers between devices  21.1 us (4%)
  local copies, waits for them, and re-layouts  16.5 us (3%)
  between operations  13.8 us (3%)
  matrix products  13.7 us (2%)
    reduce_scatter x3, waiting for transfers between devices, solve_all(): lax.psum_scatter(term(jnp.int32(0), lax.axis_size('col') * rows_dev).asty...  250 us
    reduce_scatter x3, waiting for transfers between devices, solve_all(): lax.psum_scatter(column_sums.astype(jnp.bfloat16), 'row', scatter_dimensi...  101 us
    all_gather x3, blocking collectives, solve_all(): lax.all_gather(current.astype(jnp.bfloat16), 'row', axis=0, tiled=True)  81.1 us
    all_to_all x3, waiting for transfers between devices, enter_wires(): arr_next = all_to_all(y2, ax_name, split_axis=0, concat_axis=0)  48.1 us
    all_to_all x3, starting transfers between devices, enter_wires(): arr_next = all_to_all(y2, ax_name, split_axis=0, concat_axis=0)  20.9 us
  transfers between devices with their start and end apart: 9, of which 9 were waited for; matrix products, arithmetic and copies ran while one was open for 0% of the time, Pallas kernels for 0%

profile of v1, /device:TPU:2, one launch (start us, length us, event | category | flops | bytes accessed | tf_op | source)
XLA Modules:
  0.0 547.8 jit_solution(14052164826490715267)
XLA Ops:
  6.5 0.9 fusion.66
  7.5 1.0 fusion.67
  8.6 28.6 %all_gather.9 = bf16[16,64,128]{2,1,0:T(8,128)(2,1)S(1)} all-gather(bf16[2,64,128]{2,1,0:T(8,128)(2,1)S(1)} %get-tuple-element.21), channel_id=1, replica_groups=mesh['row'=8,'col'=32] {'row'}, dimensions={0}, use_global_device_ids=true | all-gather | bytes 294912 | tf_op jit(solution)/shard_map/all_gather | solution.py:36
  37.1 0.7 fusion.62
  37.8 0.7 slice_bitcast_fusion
  38.5 0.6 gather_fusion
  39.3 1.1 convolution_convert_fusion.2
  40.4 1.7 copy.47
  42.3 84.0 %reduce-scatter.7.cloned.1.call-done = bf16[2,64,128]{2,1,0:T(8,128)(2,1)} async-done(((bf16[64,64,128]{2,1,0:T(8,128)(2,1)}), bf16[2,64,128]{2,1,0:T(8,128)(2,1)}) %reduce-scatter.7.cloned.1.call-update) | async-done | bytes 32784 | tf_op jit(solution)/shard_map/reduce_scatter | solution.py:48
  126.3 1.0 fusion.68
  127.3 26.2 %all_gather.10 = bf16[16,64,128]{2,1,0:T(8,128)(2,1)S(1)} all-gather(bf16[2,64,128]{2,1,0:T(8,128)(2,1)S(1)} %get-tuple-element.23), channel_id=1, replica_groups=mesh['row'=8,'col'=32] {'row'}, dimensions={0}, use_global_device_ids=true | all-gather | bytes 294912 | tf_op jit(solution)/shard_map/all_gather | solution.py:36
  153.5 0.6 gather_fusion.1
  154.3 1.1 convolution_convert_fusion.1
  155.4 1.7 copy.50
  157.3 83.2 %reduce-scatter.9.cloned.1.call-done = bf16[2,64,128]{2,1,0:T(8,128)(2,1)} async-done(((bf16[64,64,128]{2,1,0:T(8,128)(2,1)}), bf16[2,64,128]{2,1,0:T(8,128)(2,1)}) %reduce-scatter.9.cloned.1.call-update) | async-done | bytes 32784 | tf_op jit(solution)/shard_map/reduce_scatter | solution.py:48
  240.5 1.0 fusion.69
  241.5 26.3 %all_gather.11 = bf16[16,64,128]{2,1,0:T(8,128)(2,1)S(1)} all-gather(bf16[2,64,128]{2,1,0:T(8,128)(2,1)S(1)} %get-tuple-element.25), channel_id=1, replica_groups=mesh['row'=8,'col'=32] {'row'}, dimensions={0}, use_global_device_ids=true | all-gather | bytes 294912 | tf_op jit(solution)/shard_map/all_gather | solution.py:36
  267.8 0.6 gather_fusion.2
  268.6 1.1 convolution_convert_fusion
  269.7 1.7 copy.53
  271.5 83.2 %reduce-scatter.11.cloned.1.call-done = bf16[2,64,128]{2,1,0:T(8,128)(2,1)} async-done(((bf16[64,64,128]{2,1,0:T(8,128)(2,1)}), bf16[2,64,128]{2,1,0:T(8,128)(2,1)}) %reduce-scatter.11.cloned.1.call-update) | async-done | bytes 32784 | tf_op jit(solution)/shard_map/reduce_scatter | solution.py:48
  354.7 1.0 fusion.21
  356.0 1.2 stack.16
  357.2 6.0 %all-to-all-start = ((bf16[32,2,64,128]{3,2,1,0:T(8,128)(2,1)}), bf16[32,2,64,128]{3,2,1,0:T(8,128)(2,1)S(1)}, u32[]{:S(2)}, u32[]{:S(2)}) async-start(bf16[32,2,64,128]{3,2,1,0:T(8,128)(2,1)} %stack.16), calls=%async_computation.3 | async-start | bytes 2097152 | tf_op jit(solution)/shard_map/all_to_all | solution.py:12
  363.3 16.0 %all-to-all-done = bf16[32,2,64,128]{3,2,1,0:T(8,128)(2,1)S(1)} async-done(((bf16[32,2,64,128]{3,2,1,0:T(8,128)(2,1)}), bf16[32,2,64,128]{3,2,1,0:T(8,128)(2,1)S(1)}, u32[]{:S(2)}, u32[]{:S(2)}) %all-to-all-start) | async-done | bytes 1048608 | tf_op jit(solution)/shard_map/all_to_all | solution.py:12
  379.3 0.6 gather_fusion.3
  380.2 0.6 fusion.4
  380.8 0.8 copy.95
  381.6 35.6 %reduce-scatter.13.cloned.1.call-done = bf16[2,64,128]{2,1,0:T(8,128)(2,1)} async-done(((bf16[16,64,128]{2,1,0:T(8,128)(2,1)}), bf16[2,64,128]{2,1,0:T(8,128)(2,1)}) %reduce-scatter.13.cloned.1.call-update) | async-done | bytes 32784 | tf_op jit(solution)/shard_map/reduce_scatter | solution.py:67
  417.1 1.0 bitcast_convert_fusion.1
  418.2 1.2 stack.17
  419.4 7.4 %all-to-all-start.1 = ((bf16[32,2,64,128]{3,2,1,0:T(8,128)(2,1)}), bf16[32,2,64,128]{3,2,1,0:T(8,128)(2,1)S(1)}, u32[]{:S(2)}, u32[]{:S(2)}) async-start(bf16[32,2,64,128]{3,2,1,0:T(8,128)(2,1)} %stack.17), calls=%async_computation.5 | async-start | bytes 2097152 | tf_op jit(solution)/shard_map/all_to_all | solution.py:12
  426.9 16.1 %all-to-all-done.1 = bf16[32,2,64,128]{3,2,1,0:T(8,128)(2,1)S(1)} async-done(((bf16[32,2,64,128]{3,2,1,0:T(8,128)(2,1)}), bf16[32,2,64,128]{3,2,1,0:T(8,128)(2,1)S(1)}, u32[]{:S(2)}, u32[]{:S(2)}) %all-to-all-start.1) | async-done | bytes 1048608 | tf_op jit(solution)/shard_map/all_to_all | solution.py:12
  442.9 0.6 gather_fusion.4
  443.8 0.6 fusion.2
  444.4 0.8 copy.94
  445.2 32.9 %reduce-scatter.15.cloned.1.call-done = bf16[2,64,128]{2,1,0:T(8,128)(2,1)} async-done(((bf16[16,64,128]{2,1,0:T(8,128)(2,1)}), bf16[2,64,128]{2,1,0:T(8,128)(2,1)}) %reduce-scatter.15.cloned.1.call-update) | async-done | bytes 32784 | tf_op jit(solution)/shard_map/reduce_scatter | solution.py:67
  478.1 1.0 bitcast_convert_fusion
  479.2 1.2 stack.18
  480.4 7.4 %all-to-all-start.2 = ((bf16[32,2,64,128]{3,2,1,0:T(8,128)(2,1)}), bf16[32,2,64,128]{3,2,1,0:T(8,128)(2,1)S(1)}, u32[]{:S(2)}, u32[]{:S(2)}) async-start(bf16[32,2,64,128]{3,2,1,0:T(8,128)(2,1)} %stack.18), calls=%async_computation.7 | async-start | bytes 2097152 | tf_op jit(solution)/shard_map/all_to_all | solution.py:12
  487.9 16.1 %all-to-all-done.2 = bf16[32,2,64,128]{3,2,1,0:T(8,128)(2,1)S(1)} async-done(((bf16[32,2,64,128]{3,2,1,0:T(8,128)(2,1)}), bf16[32,2,64,128]{3,2,1,0:T(8,128)(2,1)S(1)}, u32[]{:S(2)}, u32[]{:S(2)}) %all-to-all-start.2) | async-done | bytes 1048608 | tf_op jit(solution)/shard_map/all_to_all | solution.py:12
  504.0 0.6 gather_fusion.5
  504.6 0.3 convolution_bitcast_fusion.3
  504.8 0.6 fusion
  505.4 0.8 copy.93
  506.2 33.0 %reduce-scatter.17.cloned.1.call-done = bf16[2,64,128]{2,1,0:T(8,128)(2,1)} async-done(((bf16[16,64,128]{2,1,0:T(8,128)(2,1)}), bf16[2,64,128]{2,1,0:T(8,128)(2,1)}) %reduce-scatter.17.cloned.1.call-update) | async-done | bytes 32784 | tf_op jit(solution)/shard_map/reduce_scatter | solution.py:67
  539.2 1.0 convolution_bitcast_fusion.6
  540.2 0.7 pad_maximum_fusion
  (38 shorter events, 2.0 us)
Async XLA Ops:
  6.5 32.6 %copy-start = (bf16[3,12,64,64]{3,2,1,0:T(8,128)(2,1)S(1)}, bf16[3,12,64,64]{3,2,1,0:T(8,128)(2,1)}, u32[]{:S(2)}) copy-start(bf16[3,12,64,64]{3,2,1,0:T(8,128)(2,1)} %param.5) | copy-start | bytes 884740
  6.5 119.8 %reduce-scatter.7.cloned.1.call-start = ((), (), s32[]{:S(2)}) async-start(), calls=%async_computation.9 | async-start | bytes 1081344 | tf_op jit(solution)/shard_map/reduce_scatter | solution.py:48
  42.1 84.2 %copy-start.1 = (f32[4,2,64,128]{3,2,1,0:T(8,128)S(1)}, f32[4,2,64,128]{3,2,1,0:T(8,128)}, u32[]{:S(2)}) copy-start(f32[4,2,64,128]{3,2,1,0:T(8,128)} %param.8) | copy-start | bytes 786436
  42.1 198.4 %reduce-scatter.9.cloned.1.call-start = ((), (), s32[]{:S(2)}) async-start(), calls=%async_computation.10 | async-start | bytes 1081344 | tf_op jit(solution)/shard_map/reduce_scatter | solution.py:48
  157.1 197.6 %reduce-scatter.11.cloned.1.call-start = ((), (), s32[]{:S(2)}) async-start(), calls=%async_computation.11 | async-start | bytes 1081344 | tf_op jit(solution)/shard_map/reduce_scatter | solution.py:48
  357.2 6.0 %copy-start.2 = (s32[3,12,1]{1,2,0:T(1,128)S(1)}, s32[3,12,1]{1,2,0:T(1,128)}, u32[]{:S(2)}) copy-start(s32[3,12,1]{1,2,0:T(1,128)} %param.6) | copy-start | bytes 436
  357.2 6.1 %copy-start.3 = (s32[3,12,1]{1,2,0:T(1,128)S(1)}, s32[3,12,1]{1,2,0:T(1,128)}, u32[]{:S(2)}) copy-start(s32[3,12,1]{1,2,0:T(1,128)} %param.7) | copy-start | bytes 436
  357.2 22.1 %all-to-all-start = ((bf16[32,2,64,128]{3,2,1,0:T(8,128)(2,1)}), bf16[32,2,64,128]{3,2,1,0:T(8,128)(2,1)S(1)}, u32[]{:S(2)}, u32[]{:S(2)}) async-start(bf16[32,2,64,128]{3,2,1,0:T(8,128)(2,1)} %stack.16), calls=%async_computation.3 | async-start | bytes 2097152 | tf_op jit(solution)/shard_map/all_to_all | solution.py:12
  363.2 53.9 %reduce-scatter.13.cloned.1.call-start = ((), (), s32[]{:S(2)}) async-start(), calls=%async_computation.12 | async-start | bytes 294912 | tf_op jit(solution)/shard_map/reduce_scatter | solution.py:67
  419.4 23.5 %all-to-all-start.1 = ((bf16[32,2,64,128]{3,2,1,0:T(8,128)(2,1)}), bf16[32,2,64,128]{3,2,1,0:T(8,128)(2,1)S(1)}, u32[]{:S(2)}, u32[]{:S(2)}) async-start(bf16[32,2,64,128]{3,2,1,0:T(8,128)(2,1)} %stack.17), calls=%async_computation.5 | async-start | bytes 2097152 | tf_op jit(solution)/shard_map/all_to_all | solution.py:12
  426.8 51.3 %reduce-scatter.15.cloned.1.call-start = ((), (), s32[]{:S(2)}) async-start(), calls=%async_computation.13 | async-start | bytes 294912 | tf_op jit(solution)/shard_map/reduce_scatter | solution.py:67
  480.4 23.6 %all-to-all-start.2 = ((bf16[32,2,64,128]{3,2,1,0:T(8,128)(2,1)}), bf16[32,2,64,128]{3,2,1,0:T(8,128)(2,1)S(1)}, u32[]{:S(2)}, u32[]{:S(2)}) async-start(bf16[32,2,64,128]{3,2,1,0:T(8,128)(2,1)} %stack.18), calls=%async_computation.7 | async-start | bytes 2097152 | tf_op jit(solution)/shard_map/all_to_all | solution.py:12
  487.9 51.3 %reduce-scatter.17.cloned.1.call-start = ((), (), s32[]{:S(2)}) async-start(), calls=%async_computation.14 | async-start | bytes 294912 | tf_op jit(solution)/shard_map/reduce_scatter | solution.py:67
Sparse Core Ops, SparseCore 0:
  42.2 84.0 reduce-scatter.6
  157.2 83.2 reduce-scatter.8
  271.5 83.1 reduce-scatter.10
  381.7 35.3 reduce-scatter.12
  445.3 32.7 reduce-scatter.14
  506.3 32.7 reduce-scatter.16
